TPU v7x, 128 devices: a whole 4x4x4 slice. The times are simulated.
128 devices in a mesh: group: 8 (over x, core), member: 16 (over z, y).
Axes of the slice: x: 4, y: 4, z: 4, core: 2. Of those that a mesh axis runs over, the one named last changes fastest.
Arguments:
- velocity: bfloat16 [32768, 3, 512], P(('group', 'member')), may hold values from -6 to 6
- elem_scale: float32 [32768, 3], P(('group', 'member')), may hold values from 0.05 to 0.4
- face_map: int32 [32768, 64], P(('group', 'member')), may hold values from 0 to 63, each once within a row
- ref_coords: float32 [3, 131072], P(None, ('group', 'member')), may hold values from -1 to 1
- owner_dev: int32 [131072, 1], P(('group', 'member')), may hold values from 0 to 127; in each aligned block of 1024 rows (0 to 1023, 1024 to 2047, ...) at most 16 rows name the same one
- owner_elem: int32 [131072], P(('group', 'member')), may hold values from 0 to 255
Outputs:
- grad_mean: bfloat16 [32768, 9, 512], P(('group', 'member'))
- particle_values: float32 [12, 131072], P(None, ('group', 'member'))
Inputs may be any that keep to these rules, and one draw needn't show every extreme that they name: `owner_dev`: within the rows of one device no device is named more than 16 times; that bound is reached. `face_map`: each row is a permutation of 0 to 63.
All inputs are finite; a program needn't handle non-finite values.
Results may differ from a plain program's by a relative error of at most 0.0054.
Values sent between devices are 32-bit elements; how exact they have to be, the bound alone decides.
A program may use at most 64 MiB of HBM per device.

v0:
```python
import math

import jax
import jax.numpy as jnp
import numpy as np
from jax import lax
from jax.sharding import PartitionSpec as P

EC = 256


def passed_along(shard, axis, by):
    size = lax.axis_size(axis)
    return lax.ppermute(shard, axis, [(i, (i + by) % size) for i in range(size)])


def gll_nodes():
    return -np.cos(np.pi * np.arange(8) / 7.0)


def derivative_table():
    nodes = gll_nodes()
    weights = np.array(
        [
            np.prod([nodes[first] - nodes[other] for other in range(8) if other != first])
            for first in range(8)
        ]
    )
    deriv = np.zeros((8, 8))
    for first in range(8):
        for second in range(8):
            if first != second:
                deriv[first, second] = (
                    weights[first] / weights[second] / (nodes[first] - nodes[second])
                )
            else:
                deriv[first, first] = sum(
                    (1.0 / (nodes[first] - nodes[other]) for other in range(8) if other != first)
                )
    ident = np.eye(8)
    trans = deriv.T
    blocks = [
        np.kron(np.kron(trans, ident), ident),
        np.kron(np.kron(ident, trans), ident),
        np.kron(np.kron(ident, ident), trans),
    ]
    return np.concatenate(blocks, axis=1)


def lagrange(coordinate):
    nodes = gll_nodes()
    rows = []
    for first in range(8):
        term = jnp.ones_like(coordinate)
        for second in range(8):
            if second != first:
                term = term * (
                    (coordinate - float(nodes[second])) / float(nodes[first] - nodes[second])
                )
        rows.append(term)
    return jnp.stack(rows, axis=0)


def node_weights(coords):
    along_r = lagrange(coords[0])
    along_s = lagrange(coords[1])
    along_t = lagrange(coords[2])
    table = along_r[:, None, None, :] * along_s[None, :, None, :] * along_t[None, None, :, :]
    return table.reshape(512, coords.shape[1])


def per_device(velocity, elem_scale, face_map, ref_coords, owner_dev, owner_elem):
    element_count = velocity.shape[0]
    cross = EC
    table = jnp.asarray(derivative_table().astype(np.float32)).astype(jnp.bfloat16)
    raw_grad = jnp.dot(
        velocity.reshape(element_count * 3, 512), table, preferred_element_type=jnp.float32
    )
    raw_grad = (raw_grad.reshape(element_count, 3, 3, 512) * elem_scale[:, None, :, None]).reshape(
        element_count, 9, 512
    )
    corner = raw_grad.reshape(element_count, 9, 64, 8)
    bottom = corner[..., 0]
    top_faces = corner[..., 7]
    matcher = (face_map[:, :, None] == lax.broadcasted_iota(jnp.int32, (1, 1, 64), 2)).astype(
        jnp.float32
    )
    bottom_turned = jnp.einsum("ecf,efm->ecm", bottom, matcher, precision=lax.Precision.HIGHEST)
    prior_top = passed_along(top_faces, ("group", "member"), 1)
    next_bottom = passed_along(bottom_turned, ("group", "member"), -1)
    top_prior = jnp.concatenate([prior_top, top_faces[: element_count - cross]], axis=0)
    matched_top = jnp.einsum("ecg,efg->ecf", top_prior, matcher, precision=lax.Precision.HIGHEST)
    bottom_mean = 0.5 * (bottom + matched_top)
    top_mean = 0.5 * (top_faces + jnp.concatenate([bottom_turned[cross:], next_bottom], axis=0))
    position = lax.broadcasted_iota(jnp.int32, (1, 1, 512), 2) % 8
    low_full = jnp.repeat(bottom_mean, 8, axis=2)
    high_full = jnp.repeat(top_mean, 8, axis=2)
    grad_mean = jnp.where(
        position == 0, low_full, jnp.where(position == 7, high_full, raw_grad)
    ).astype(jnp.bfloat16)
    fields = jnp.concatenate([velocity, grad_mean], axis=1)
    parts = owner_elem.shape[0]
    device_count = lax.axis_size(("group", "member"))
    capacity = 2 * parts // device_count
    target = owner_dev[:, 0]
    width = math.gcd(parts, 512)
    rounds = parts // width
    one_hot = (
        target.reshape(rounds, width)[:, :, None]
        == jnp.arange(device_count, dtype=jnp.int32)[None, None, :]
    ).astype(jnp.float32)
    strict_lower = (
        lax.broadcasted_iota(jnp.int32, (width, width), 0)
        > lax.broadcasted_iota(jnp.int32, (width, width), 1)
    ).astype(jnp.float32)

    def tally(running, hot_block):
        earlier = (
            jnp.dot(strict_lower, hot_block, precision=lax.Precision.HIGHEST) + running[None, :]
        )
        ranks = jnp.sum(earlier * hot_block, axis=1)
        return (running + jnp.sum(hot_block, axis=0), ranks)

    _, ranks = lax.scan(tally, jnp.zeros((device_count,), jnp.float32), one_hot)
    slots = target * capacity + ranks.reshape(parts).astype(jnp.int32)
    payload = jnp.concatenate([ref_coords, owner_elem.astype(jnp.float32)[None, :]], axis=0)
    buffer = jnp.zeros((4, device_count * capacity), jnp.float32).at[:, slots].set(payload)
    received = lax.all_to_all(
        buffer.reshape(4, device_count, capacity),
        ("group", "member"),
        split_axis=1,
        concat_axis=1,
        tiled=True,
    )
    sources = received.shape[1]
    depth = received.shape[2]
    block_count = sources // 8
    blocked = received.reshape(4, block_count, sources // block_count * depth).transpose(1, 0, 2)

    def serve_block(portion):
        element_ids = portion[3].astype(jnp.int32)
        weights = node_weights(portion[:3])
        gathered = fields[element_ids].astype(jnp.float32)
        return jnp.einsum("bcn,nb->cb", gathered, weights, precision=lax.Precision.HIGHEST)

    results = lax.map(serve_block, blocked)
    answered = lax.all_to_all(
        results.transpose(1, 0, 2).reshape(12, sources, depth),
        ("group", "member"),
        split_axis=1,
        concat_axis=1,
        tiled=True,
    )
    particle_values = answered.reshape(12, device_count * capacity)[:, slots]
    return (grad_mean, particle_values)


def solution(mesh):
    in_specs = (
        P(("group", "member"), None, None),
        P(("group", "member"), None),
        P(("group", "member"), None),
        P(None, ("group", "member")),
        P(("group", "member"), None),
        P(("group", "member")),
    )
    out_specs = (P(("group", "member"), None, None), P(None, ("group", "member")))
    return jax.shard_map(
        per_device, mesh=mesh, in_specs=in_specs, out_specs=out_specs, check_vma=False
    )
```

profile of v0, /device:TPU:1, one launch (start us, length us, event | category | flops | bytes accessed | tf_op | source)
XLA Modules:
  0.0 180.6 jit_solution(3320335212543174341)
XLA Ops:
  0.6 3.1 %bitcast_multiply_fusion = f32[256,3,3,512]{0,3,1,2:T(8,128)S(1)} fusion(f32[256,3]{0,1:T(4,128)} %param.12, bf16[3,512,512,1]{2,1,3,0:T(8,128)(2,1)} %constant.629, bf16[256,3,512]{2,0,1:T(8,128)(2,1)} %param.11), kind=kOutput, calls=%fused_computation.77 | convolution fusion | flops 1209139200 | bytes 7080960 | tf_op jit(solution)/shard_map/dot_general | solution.py:76
  12.6 7.5 %fusion.10 = f32[256,9,64]{2,1,0:T(8,128)S(1)} fusion(s32[256,64]{1,0:T(8,128)S(1)} %copy.58, f32[256,9,64,1]{2,1,0,3:T(8,128)} %copy.87), kind=kOutput, calls=%fused_computation.72 | convolution fusion | flops 114294784 | bytes 1245184 | tf_op jit(solution)/shard_map/ecf,efm->ecm/dot_general | solution.py:88
  21.7 5.5 %collective-permute-start.1 = (f32[256,9,64]{0,2,1:T(8,128)}, f32[256,9,64]{0,2,1:T(8,128)}, u32[]{:S(2)}, u32[]{:S(2)}) collective-permute-start(f32[256,9,64]{0,2,1:T(8,128)} %copy.62), channel_id=1, source_target_pairs={{0,127},{1,0},{2,1},{3,2},{4,3},{5,4},{6,5},{7,6},{8,7},{9,8},{10,... | collective-permute-start | bytes 1769480 | tf_op jit(solution)/shard_map/ppermute | solution.py:14
  30.9 3.3 %scatter_custom_fusion = f32[4,2048]{0,1:T(8,128)S(1)} fusion(s32[1024]{0:T(1024)S(1)} %bitcast.161, f32[1024,4]{1,0:T(8,128)S(1)} %copy.65, f32[]{:T(128)} %constant.621.clone.1), kind=kCustom, calls=%fused_computation.89 | custom fusion | bytes 32772 | tf_op jit(solution)/shard_map/scatter | solution.py:127
  35.8 6.5 %all-to-all-start = ((f32[4,128,16]{2,0,1:T(4,128)}), f32[4,128,16]{2,0,1:T(4,128)}, u32[]{:S(2)}, u32[]{:S(2)}) async-start(f32[4,128,16]{2,0,1:T(4,128)} %copy.66), calls=%async_computation | async-start | bytes 524288 | tf_op jit(solution)/shard_map/all_to_all | solution.py:128
  42.3 3.5 %copy.63 = bf16[256,3,3,512]{3,0,2,1:T(8,128)(2,1)S(1)} copy(f32[256,3,3,512]{0,3,1,2:T(8,128)} %copy-done) | data formatting | bytes 7077888 | tf_op jit(solution)/shard_map/mul | solution.py:79
  50.4 3.0 %all-to-all-done = f32[4,128,16]{2,0,1:T(4,128)} async-done(((f32[4,128,16]{2,0,1:T(4,128)}), f32[4,128,16]{2,0,1:T(4,128)}, u32[]{:S(2)}, u32[]{:S(2)}) %all-to-all-start) | async-done | bytes 32800 | tf_op jit(solution)/shard_map/all_to_all | solution.py:128
  57.5 8.7 %fusion.11 = f32[256,9,64]{2,1,0:T(8,128)} fusion(f32[256,9,64]{2,1,0:T(8,128)S(1)} %copy.59, s32[256,64]{1,0:T(8,128)S(1)} %copy-done.6), kind=kOutput, calls=%fused_computation.73 | convolution fusion | flops 114294784 | bytes 1245184 | tf_op jit(solution)/shard_map/ecg,efg->ecf/dot_general | solution.py:92
  66.3 3.1 %copy.60 = f32[256,9,64]{0,2,1:T(8,128)} copy(f32[256,9,64]{2,1,0:T(8,128)} %fusion.11) | data formatting | bytes 1179648 | tf_op jit(solution)/shard_map/ecg,efg->ecf/dot_general | solution.py:92
  74.5 5.7 %copy.70 = bf16[256,12,512]{2,1,0:T(8,128)(2,1)} copy(bf16[256,12,512]{0,2,1:T(8,128)(2,1)S(1)} %pad_maximum_fusion) | data formatting | bytes 6291456 | tf_op jit(solution)/shard_map/while | solution.py:146
  80.2 73.1 %while.26 = (s32[]{:T(128)}, f32[16,12,128]{2,1,0:T(8,128)S(1)}, f32[16,4,128]{2,0,1:T(8,128)}, bf16[256,12,512]{2,1,0:T(8,128)(2,1)}, s32[]{:T(128)}) while((s32[]{:T(128)}, f32[16,12,128]{2,1,0:T(8,128)S(1)}, f32[16,4,128]{2,0,1:T(8,128)}, bf16[256,12,512]{2,1,0:T(8,128)(2,1)}, s32[]{:T(128)}) %tuple.96), condition=%wide.region_6.7_spmd, body=%wide.region_5.6_spmd.sunk | while | flops 2478850 | bytes 5930053 | solution.py:146
  81.3 2.9 %gather_fusion = bf16[128,12,512]{2,1,0:T(8,128)(2,1)S(1)} fusion(bf16[256,12,512]{2,1,0:T(8,128)(2,1)} %get-tuple-element.368, s32[1024]{0:T(1024)S(1)} %pad_clamp_fusion.2), kind=kCustom, calls=%fused_computation.clone.1 | custom fusion | bytes 3146240 | tf_op jit(solution)/shard_map/while/body/eval_jaxpr/gather | solution.py:143
  85.8 2.9 %gather_fusion = bf16[128,12,512]{2,1,0:T(8,128)(2,1)S(1)} fusion(bf16[256,12,512]{2,1,0:T(8,128)(2,1)} %get-tuple-element.368, s32[1024]{0:T(1024)S(1)} %pad_clamp_fusion.2), kind=kCustom, calls=%fused_computation.clone.1 | custom fusion | bytes 3146240 | tf_op jit(solution)/shard_map/while/body/eval_jaxpr/gather | solution.py:143
  90.4 2.9 %gather_fusion = bf16[128,12,512]{2,1,0:T(8,128)(2,1)S(1)} fusion(bf16[256,12,512]{2,1,0:T(8,128)(2,1)} %get-tuple-element.368, s32[1024]{0:T(1024)S(1)} %pad_clamp_fusion.2), kind=kCustom, calls=%fused_computation.clone.1 | custom fusion | bytes 3146240 | tf_op jit(solution)/shard_map/while/body/eval_jaxpr/gather | solution.py:143
  95.0 2.9 %gather_fusion = bf16[128,12,512]{2,1,0:T(8,128)(2,1)S(1)} fusion(bf16[256,12,512]{2,1,0:T(8,128)(2,1)} %get-tuple-element.368, s32[1024]{0:T(1024)S(1)} %pad_clamp_fusion.2), kind=kCustom, calls=%fused_computation.clone.1 | custom fusion | bytes 3146240 | tf_op jit(solution)/shard_map/while/body/eval_jaxpr/gather | solution.py:143
  99.6 2.9 %gather_fusion = bf16[128,12,512]{2,1,0:T(8,128)(2,1)S(1)} fusion(bf16[256,12,512]{2,1,0:T(8,128)(2,1)} %get-tuple-element.368, s32[1024]{0:T(1024)S(1)} %pad_clamp_fusion.2), kind=kCustom, calls=%fused_computation.clone.1 | custom fusion | bytes 3146240 | tf_op jit(solution)/shard_map/while/body/eval_jaxpr/gather | solution.py:143
  104.1 2.9 %gather_fusion = bf16[128,12,512]{2,1,0:T(8,128)(2,1)S(1)} fusion(bf16[256,12,512]{2,1,0:T(8,128)(2,1)} %get-tuple-element.368, s32[1024]{0:T(1024)S(1)} %pad_clamp_fusion.2), kind=kCustom, calls=%fused_computation.clone.1 | custom fusion | bytes 3146240 | tf_op jit(solution)/shard_map/while/body/eval_jaxpr/gather | solution.py:143
  108.7 2.9 %gather_fusion = bf16[128,12,512]{2,1,0:T(8,128)(2,1)S(1)} fusion(bf16[256,12,512]{2,1,0:T(8,128)(2,1)} %get-tuple-element.368, s32[1024]{0:T(1024)S(1)} %pad_clamp_fusion.2), kind=kCustom, calls=%fused_computation.clone.1 | custom fusion | bytes 3146240 | tf_op jit(solution)/shard_map/while/body/eval_jaxpr/gather | solution.py:143
  113.3 2.9 %gather_fusion = bf16[128,12,512]{2,1,0:T(8,128)(2,1)S(1)} fusion(bf16[256,12,512]{2,1,0:T(8,128)(2,1)} %get-tuple-element.368, s32[1024]{0:T(1024)S(1)} %pad_clamp_fusion.2), kind=kCustom, calls=%fused_computation.clone.1 | custom fusion | bytes 3146240 | tf_op jit(solution)/shard_map/while/body/eval_jaxpr/gather | solution.py:143
  136.1 2.9 %gather_fusion = bf16[128,12,512]{2,1,0:T(8,128)(2,1)S(1)} fusion(bf16[256,12,512]{2,1,0:T(8,128)(2,1)} %get-tuple-element.368, s32[1024]{0:T(1024)S(1)} %pad_clamp_fusion.2), kind=kCustom, calls=%fused_computation.clone.1 | custom fusion | bytes 3146240 | tf_op jit(solution)/shard_map/while/body/eval_jaxpr/gather | solution.py:143
  140.7 2.9 %gather_fusion = bf16[128,12,512]{2,1,0:T(8,128)(2,1)S(1)} fusion(bf16[256,12,512]{2,1,0:T(8,128)(2,1)} %get-tuple-element.368, s32[1024]{0:T(1024)S(1)} %pad_clamp_fusion.2), kind=kCustom, calls=%fused_computation.clone.1 | custom fusion | bytes 3146240 | tf_op jit(solution)/shard_map/while/body/eval_jaxpr/gather | solution.py:143
  145.3 2.9 %gather_fusion = bf16[128,12,512]{2,1,0:T(8,128)(2,1)S(1)} fusion(bf16[256,12,512]{2,1,0:T(8,128)(2,1)} %get-tuple-element.368, s32[1024]{0:T(1024)S(1)} %pad_clamp_fusion.2), kind=kCustom, calls=%fused_computation.clone.1 | custom fusion | bytes 3146240 | tf_op jit(solution)/shard_map/while/body/eval_jaxpr/gather | solution.py:143
  157.2 6.9 %all-to-all-start.1 = ((f32[128,1,192]{2,1,0:T(1,128)}), f32[128,1,192]{2,1,0:T(1,128)S(1)}, u32[]{:S(2)}, u32[]{:S(2)}) async-start(f32[128,1,192]{2,1,0:T(1,128)} %reshape.2830), calls=%async_computation.1 | async-start | bytes 262144 | tf_op jit(solution)/shard_map/all_to_all | solution.py:147
  166.7 7.7 %all-to-all-done.1 = f32[128,1,192]{2,1,0:T(1,128)S(1)} async-done(((f32[128,1,192]{2,1,0:T(1,128)}), f32[128,1,192]{2,1,0:T(1,128)S(1)}, u32[]{:S(2)}, u32[]{:S(2)}) %all-to-all-start.1) | async-done | bytes 98336 | tf_op jit(solution)/shard_map/all_to_all | solution.py:147
  (307 shorter events, 84.9 us)
Async XLA Ops:
  3.7 2.1 %copy-start = (f32[256,3,3,512]{0,3,1,2:T(8,128)}, f32[256,3,3,512]{0,3,1,2:T(8,128)S(1)}, u32[]{:S(2)}) copy-start(f32[256,3,3,512]{0,3,1,2:T(8,128)S(1)} %bitcast_multiply_fusion) | copy-start | bytes 14155780
  5.8 3.9 %copy-start.8 = (s32[256,64]{0,1:T(8,128)S(1)}, s32[256,64]{0,1:T(8,128)}, u32[]{:S(2)}) copy-start(s32[256,64]{0,1:T(8,128)} %param.13) | copy-start | bytes 196612
  7.7 47.5 %collective-permute-start = (f32[256,9,64]{0,2,1:T(8,128)}, f32[256,9,64]{0,2,1:T(8,128)}, u32[]{:S(2)}, u32[]{:S(2)}) collective-permute-start(f32[256,9,64]{0,2,1:T(8,128)} %bitcast.123), channel_id=1, source_target_pairs={{0,1},{1,2},{2,3},{3,4},{4,5},{5,6},{6,7},{7,8},{8,9},{9,10},{10,1... | collective-permute-start | bytes 1769480 | tf_op jit(solution)/shard_map/ppermute | solution.py:14
  9.9 10.3 %copy-start.5 = (s32[256,64]{1,0:T(8,128)}, s32[256,64]{1,0:T(8,128)S(1)}, u32[]{:S(2)}) copy-start(s32[256,64]{1,0:T(8,128)S(1)} %copy.58) | copy-start | bytes 196612
  20.2 7.5 %copy-start.9 = (s32[1024,1]{0,1:T(1,128)S(1)}, s32[1024,1]{0,1:T(1,128)}, u32[]{:S(2)}) copy-start(s32[1024,1]{0,1:T(1,128)} %param.15) | copy-start | bytes 12292
  21.7 48.9 %collective-permute-start.1 = (f32[256,9,64]{0,2,1:T(8,128)}, f32[256,9,64]{0,2,1:T(8,128)}, u32[]{:S(2)}, u32[]{:S(2)}) collective-permute-start(f32[256,9,64]{0,2,1:T(8,128)} %copy.62), channel_id=1, source_target_pairs={{0,127},{1,0},{2,1},{3,2},{4,3},{5,4},{6,5},{7,6},{8,7},{9,8},{10,... | collective-permute-start | bytes 1769480 | tf_op jit(solution)/shard_map/ppermute | solution.py:14
  28.4 2.2 %copy-start.11 = (s32[1024]{0:T(1024)S(1)}, s32[1024]{0:T(1024)}, u32[]{:S(2)}) copy-start(s32[1024]{0:T(1024)} %param.16) | copy-start | bytes 12292
  28.4 2.2 %copy-start.10 = (f32[3,1024]{1,0:T(4,128)S(1)}, f32[3,1024]{1,0:T(4,128)}, u32[]{:S(2)}) copy-start(f32[3,1024]{1,0:T(4,128)} %param.14) | copy-start | bytes 36868
  35.8 17.7 %all-to-all-start = ((f32[4,128,16]{2,0,1:T(4,128)}), f32[4,128,16]{2,0,1:T(4,128)}, u32[]{:S(2)}, u32[]{:S(2)}) async-start(f32[4,128,16]{2,0,1:T(4,128)} %copy.66), calls=%async_computation | async-start | bytes 524288 | tf_op jit(solution)/shard_map/all_to_all | solution.py:128
  50.4 7.1 %copy-start.6 = (s32[256,64]{1,0:T(8,128)S(1)}, s32[256,64]{1,0:T(8,128)}, u32[]{:S(2)}) copy-start(s32[256,64]{1,0:T(8,128)} %copy-done.5) | copy-start | bytes 196612
  66.3 5.4 %copy-start.3 = (bf16[256,9,512]{0,2,1:T(8,128)(2,1)S(1)}, bf16[256,9,512]{0,2,1:T(8,128)(2,1)}, u32[]{:S(2)}) copy-start(bf16[256,9,512]{0,2,1:T(8,128)(2,1)} %copy.64) | copy-start | bytes 7077892
  71.7 2.5 %copy-start.4 = (bf16[256,3,512]{0,2,1:T(8,128)(2,1)S(1)}, bf16[256,3,512]{0,2,1:T(8,128)(2,1)}, u32[]{:S(2)}) copy-start(bf16[256,3,512]{0,2,1:T(8,128)(2,1)} %copy.68) | copy-start | bytes 2359300
  72.8 1.4 copy-start.1
  74.5 5.7 %copy-start.7 = (f32[16,12,128]{2,1,0:T(8,128)S(1)}, f32[16,12,128]{2,1,0:T(8,128)}, u32[]{:S(2)}) copy-start(f32[16,12,128]{2,1,0:T(8,128)} %custom-call.5) | copy-start | bytes 294916
  153.3 10.9 %copy-start.2 = (bf16[256,9,512]{0,2,1:T(8,128)(2,1)S(1)}, bf16[256,9,512]{0,2,1:T(8,128)(2,1)}, u32[]{:S(2)}) copy-start(bf16[256,9,512]{0,2,1:T(8,128)(2,1)} %copy-done.1) | copy-start | bytes 7077892
  157.2 17.1 %all-to-all-start.1 = ((f32[128,1,192]{2,1,0:T(1,128)}), f32[128,1,192]{2,1,0:T(1,128)S(1)}, u32[]{:S(2)}, u32[]{:S(2)}) async-start(f32[128,1,192]{2,1,0:T(1,128)} %reshape.2830), calls=%async_computation.1 | async-start | bytes 262144 | tf_op jit(solution)/shard_map/all_to_all | solution.py:147
where the time goes:
time: 183 us; the launch traced here: 181 us
  local copies, waits for them, and re-layouts  110 us (60%)
  matrix products  21.1 us (12%)
  starting transfers between devices  21 us (11%)
  other arithmetic  15.7 us (9%)
  waiting for transfers between devices  10.7 us (6%)
    gather x16, local copies, waits for them, and re-layouts, serve_block(): gathered = fields[element_ids].astype(jnp.float32)  45.9 us
    dynamic_slice x16, local copies, waits for them, and re-layouts, per_device(): results = lax.map(serve_block, blocked)  11.9 us
    unnamed x33, local copies, waits for them, and re-layouts  11.7 us
    dot_general x1, matrix products, per_device(): jnp.einsum('ecg,efg->ecf', top_prior, matcher, precision=lax.Precision.HI...  8.75 us
    while x16, other arithmetic  8.35 us
    all_to_all x1, waiting for transfers between devices, per_device(): lax.all_to_all(results.transpose(1, 0, 2).reshape(12, sources, depth), ('...  7.72 us
    ppermute x2, starting transfers between devices, passed_along(): lax.ppermute(shard, axis, [(i, (i + by) % size) for i in range(size)])  7.6 us
    dot_general x1, matrix products, per_device(): jnp.einsum('ecf,efm->ecm', bottom, matcher, precision=lax.Precision.HIGHEST)  7.52 us
  transfers between devices with their start and end apart: 4, of which 2 were waited for; matrix products, arithmetic and copies ran while one was open for 27% of the time, Pallas kernels for 0%

commit v1 on v0

v1 whole, which is shorter than its diff:
```python
import functools

import jax
import jax.numpy as jnp
import numpy as np
from jax import lax
from jax.experimental import pallas as pl
from jax.experimental.pallas import tpu as pltpu
from jax.sharding import PartitionSpec as P

MESH = pl.DeviceIdType.MESH
F32, BF16 = jnp.float32, jnp.bfloat16
NDEV, CAP = 128, 16


def gll_nodes():
    return -np.cos(np.pi * np.arange(8) / 7.0)


def deriv_matrix():
    nodes = gll_nodes()
    weights = np.array([np.prod([nodes[a] - nodes[b] for b in range(8) if b != a]) for a in range(8)])
    deriv = np.zeros((8, 8))
    for a in range(8):
        for b in range(8):
            if a != b:
                deriv[a, b] = weights[a] / weights[b] / (nodes[a] - nodes[b])
            else:
                deriv[a, a] = sum(1.0 / (nodes[a] - nodes[o]) for o in range(8) if o != a)
    return deriv


def tables():
    dt = deriv_matrix().astype(np.float32).T
    eye = np.eye(8, dtype=np.float32)
    gr = np.kron(np.kron(dt, eye), eye)
    gs = np.kron(np.kron(eye, dt), eye)
    gt = np.kron(np.kron(eye, eye), dt)
    low = 8 * np.arange(64)
    ident = np.eye(512, dtype=np.float32)
    face = np.concatenate([ident[:, low + 7], gt[:, low + 7], ident[:, low], gt[:, low]], axis=1)
    fr, fs = np.kron(dt, eye), np.kron(eye, dt)
    inner = np.zeros((256, 256), np.float32)
    inner[0:64, 0:64] = fr
    inner[128:192, 64:128] = fr
    inner[0:64, 128:192] = fs
    inner[128:192, 192:256] = fs
    block = np.concatenate([gs[:256, :256], gt[:256, :256]], axis=1)
    upper = np.triu(np.ones((128, 128), np.float32), 1)
    count = np.concatenate([upper, np.ones((128, 128), np.float32)], axis=1)
    return [jnp.asarray(t, BF16) for t in (face, gr, block, inner, count)]


def rounded_deriv():
    return deriv_matrix().astype(np.float32).astype(jnp.dtype(BF16)).astype(np.float32)


def split3(x):
    hi = x.astype(BF16)
    rest = x - hi.astype(F32)
    mid = rest.astype(BF16)
    return hi, mid, (rest - mid.astype(F32)).astype(BF16)


def dot(a, b):
    return jnp.dot(a, b, preferred_element_type=F32)


def dot_t(a, b):
    return lax.dot_general(a, b, (((1,), (1,)), ((), ())), preferred_element_type=F32)


def iota(shape, axis):
    return lax.broadcasted_iota(jnp.int32, shape, axis)


def take_lanes(x, idx):
    return jnp.take_along_axis(x, idx, axis=1, mode="promise_in_bounds")


def column(values):
    row = iota((8, 1), 0)
    out = jnp.full((8, 1), float(values[0]), F32)
    for a in range(1, 8):
        out = jnp.where(row == a, float(values[a]), out)
    return out


def lagrange(y):
    nodes = gll_nodes()
    row = iota(y.shape, 0)
    out = None
    for b in range(8):
        inv = column([1.0 / (nodes[a] - nodes[b]) if a != b else 0.0 for a in range(8)])
        term = jnp.where(row == b, 1.0, (y - float(nodes[b])) * inv)
        out = term if out is None else out * term
    return out


def kernel(v, sc, fm, rc, od, oe, face, gr, block, inner, count, dtab,
           grad, pv,
           topm, botm, rtop, rbot, scp, scn, invs, invr, sreq, rreq, sret, rret,
           scols, vt, hot, zs, zt, res, wts, rj, hot2, sclanes, rt, fmt,
           hs, hr, qs, qr, ps, pr, sem_a, sem_b):
    g, m = lax.axis_index("group"), lax.axis_index("member")
    me = g * 16 + m
    z, y = m // 4, m % 4
    nxt, prv = (me + 1) % NDEV, (me + NDEV - 1) % NDEV
    nxt, prv = (nxt // 16, nxt % 16), (prv // 16, prv % 16)

    bar = pltpu.get_barrier_semaphore()
    partners = [nxt, prv] + [((g + i) % 8, m) for i in range(1, 8)]
    zpart = [(g, ((z + i) % 4) * 4 + y) for i in range(1, 4)]
    ypart = [(g, z * 4 + (y + i) % 4) for i in range(1, 4)]
    for p in partners + zpart + ypart:
        pl.semaphore_signal(bar, inc=1, device_id=p, device_id_type=MESH)

    for c in range(3):
        x = dot(v[c], face[...])
        topm[c] = x[:, :128]
        botm[c] = x[:, 128:]

    fmt[0:64, :] = fm[:, 0:128].astype(F32)
    fmt[64:128, :] = fm[:, 128:256].astype(F32)

    def invert(f, acc):
        lo, hi = acc
        where = iota((64, 128), 0).astype(F32)
        value = f.astype(F32)
        lo = jnp.where(fmt[pl.ds(f, 1), :] == where, value, lo)
        hi = jnp.where(fmt[pl.ds(64 + f, 1), :] == where, value, hi)
        return lo, hi

    zero = jnp.zeros((64, 128), F32)
    inv_lo, inv_hi = lax.fori_loop(0, 64, invert, (zero, zero), unroll=8)
    invs[...] = jnp.concatenate([inv_lo, inv_hi], axis=0).T.astype(jnp.int32)

    running = jnp.zeros((128, 128), F32)
    for b in range(8):
        lanes = slice(128 * b, 128 * b + 128)
        hit = (iota((128, 128), 0) == od[:, lanes]).astype(F32)
        hit16 = hit.astype(BF16)
        hot2[0:128, lanes] = hit16
        hot2[128:256, lanes] = hit16
        before = dot(hit16, count[...])
        rank = jnp.sum(hit * (before[:, :128] + running), axis=0, keepdims=True)
        running = running + before[:, 128:]
        rj[:, lanes] = (iota((16, 128), 0).astype(F32) == rank).astype(F32)
    rows = [rc[i : i + 1, :] for i in range(3)] + [oe[...].astype(F32)]
    spread = jnp.concatenate([rj[...] * row for row in rows] + [jnp.zeros((64, 1024), F32)], axis=0)
    send = None
    for part in split3(spread):
        one = dot_t(hot2[0:128, :], part)
        send = one if send is None else send + one
    sreq[:, 0, :] = send

    pl.semaphore_wait(bar, len(partners) + 6)
    for p in zpart:
        pl.semaphore_signal(sem_a, inc=1, device_id=p, device_id_type=MESH)

    def push(src, dst, k, to):
        copy = pltpu.make_async_remote_copy(
            src_ref=src, dst_ref=dst, send_sem=hs.at[k], recv_sem=hr.at[k], device_id=to, device_id_type=MESH
        )
        copy.start()
        return copy

    halo = [push(sc, scp, 0, nxt), push(sc, scn, 1, prv), push(invs, invr, 2, prv)]
    for c in range(3):
        halo.append(push(topm.at[c], rtop.at[c], 3 + 2 * c, nxt))
        halo.append(push(botm.at[c], rbot.at[c], 4 + 2 * c, prv))

    pl.semaphore_wait(sem_a, 3)
    for p in ypart:
        pl.semaphore_signal(sem_b, inc=1, device_id=p, device_id_type=MESH)
    pl.semaphore_wait(sem_b, 3)

    def exchange(src, dst, ssem, rsem):
        pltpu.make_async_copy(src.at[me], dst.at[me], rsem).start()

        def one(i, carry):
            t = (me + i) % NDEV
            pltpu.make_async_remote_copy(
                src_ref=src.at[t], dst_ref=dst.at[me], send_sem=ssem, recv_sem=rsem,
                device_id=(t // 16, t % 16), device_id_type=MESH,
            ).start()
            return carry

        lax.fori_loop(1, NDEV, one, 0)

    exchange(sreq, rreq, qs, qr)

    for c in range(3):
        vt[c] = v[c].astype(F32).T.astype(BF16)
    for d in range(3):
        for i, part in enumerate(split3(sc[d : d + 1, :])):
            sclanes[3 * d + i : 3 * d + i + 1, :] = part.astype(F32)
    scales16 = jnp.concatenate([sclanes[0:9, :], jnp.zeros((7, 256), F32)], axis=0).astype(BF16)

    pltpu.make_async_copy(rreq, rreq, qr).wait()
    rt[...] = rreq[:, 0, :].T

    half = column([0.5] + [1.0] * 6 + [0.5])
    dr = [dtab[:, 128 * a : 128 * a + 1] for a in range(8)]

    def pair(row, j):
        return jnp.concatenate([rt[pl.ds(row + 2 * j, 1), :], rt[pl.ds(row + 2 * j + 1, 1), :]], axis=1)

    def put(cc, j, val, add):
        for h in range(2):
            part = val[:, 128 * h : 128 * h + 128]
            row = pl.ds(cc * 16 + 2 * j + h, 1)
            res[row, :] = res[row, :] + part if add else part

    def own(j, carry):
        lanes = pl.ds(pl.multiple_of(j * 256, 256), 256)
        lag, der = [], []
        for a in range(3):
            base = lagrange(jnp.broadcast_to(pair(16 * a, j), (8, 256)))
            wts[8 * a : 8 * a + 8, lanes] = base
            lag.append(base)
            use = base * half if a == 2 else base
            total = None
            for b in range(8):
                term = use[b : b + 1, :] * dr[b]
                total = term if total is None else total + term
            der.append(total)
        hit = (iota((256, 256), 0).astype(F32) == pair(48, j)).astype(F32).astype(BF16)
        hot[:, lanes] = hit
        pieces = dot(scales16, hit)
        ht = lag[2] * half
        for c in range(3):
            picked = dot(vt[c], hit)
            s0 = s1 = s2 = jnp.zeros((8, 256), F32)
            for jj in range(8):
                a0 = a1 = jnp.zeros((8, 256), F32)
                for i in range(8):
                    x = picked[64 * i + 8 * jj : 64 * i + 8 * jj + 8, :]
                    a0 = a0 + lag[0][i : i + 1, :] * x
                    a1 = a1 + der[0][i : i + 1, :] * x
                s0 = s0 + lag[1][jj : jj + 1, :] * a0
                s1 = s1 + der[1][jj : jj + 1, :] * a0
                s2 = s2 + lag[1][jj : jj + 1, :] * a1
            put(c, j, jnp.sum(lag[2] * s0, axis=0, keepdims=True), False)
            for d, part in enumerate((ht * s2, ht * s1, der[2] * s0)):
                scale = pieces[3 * d : 3 * d + 1] + pieces[3 * d + 1 : 3 * d + 2] + pieces[3 * d + 2 : 3 * d + 3]
                put(3 + 3 * c + d, j, jnp.sum(part, axis=0, keepdims=True) * scale, False)
        return carry

    lax.fori_loop(0, 8, own, 0)

    for k in range(3):
        halo[k].wait_recv()
    scols[...] = jnp.zeros((128, 128), F32)
    for h in range(2):
        lanes = slice(128 * h, 128 * h + 128)
        scols[8 * h : 8 * h + 3, :] = scp[:, lanes]
        scols[16 + 8 * h : 16 + 8 * h + 3, :] = scn[:, lanes]
        scols[32 + 8 * h : 32 + 8 * h + 3, :] = sc[:, lanes]
    cols = scols[...].T

    def scale_col(base, d):
        first = cols[:, base + d : base + d + 1]
        second = cols[:, base + 8 + d : base + 8 + d + 1]
        return jnp.concatenate([jnp.broadcast_to(first, (128, 128)), jnp.broadcast_to(second, (128, 128))], axis=0)

    left = iota((256, 128), 1) < 64
    both = [jnp.where(left, scale_col(0, d), scale_col(16, d)) for d in range(3)]
    fm2, inv2 = fmt[...].T.astype(jnp.int32), invr[...]
    left2 = iota((128, 128), 1) < 64
    idx = jnp.concatenate(
        [
            jnp.where(left2, fm2, 64 + pltpu.roll(inv2, 64, 1)),
            jnp.where(left2, pltpu.roll(fm2, 64, 1), 64 + inv2),
        ],
        axis=0,
    )

    for c in range(3):
        halo[3 + 2 * c].wait_recv()
        halo[4 + 2 * c].wait_recv()
        up, down = rtop[c], rbot[c]
        rs = dot(jnp.concatenate([up, down], axis=1).astype(BF16), inner[...])
        fields = [rs[:, :128], rs[:, 128:], jnp.where(left, pltpu.roll(up, 64, 1), down)]
        for d in range(3):
            turned = take_lanes(fields[d] * both[d], idx)
            zs[3 * c + d] = turned
            zt[128 * d : 128 * d + 128, :] = turned.T.astype(BF16)

        def neighbours(j, carry):
            lanes = pl.ds(pl.multiple_of(j * 256, 256), 256)
            picked = dot(zt[...], hot[:, lanes])
            lr, ls, lt = wts[0:8, lanes], wts[8:16, lanes], wts[16:24, lanes]
            for d in range(3):
                lo = hi = jnp.zeros((8, 256), F32)
                for i in range(8):
                    at = 128 * d + 8 * i
                    lo = lo + lr[i : i + 1, :] * picked[at : at + 8, :]
                    hi = hi + lr[i : i + 1, :] * picked[at + 64 : at + 72, :]
                both_faces = 0.5 * (lt[0:1, :] * lo + lt[7:8, :] * hi)
                put(3 + 3 * c + d, j, jnp.sum(ls * both_faces, axis=0, keepdims=True), True)
            return carry

        lax.fori_loop(0, 8, neighbours, 0)

    res[192:256, :] = jnp.zeros((64, 128), F32)
    sret[:, 0, :] = res[0:128, :].T
    sret[:, 1, :] = res[128:256, :].T
    exchange(sret, rret, ps, pr)

    spot = iota((256, 128), 1)
    on_face = (spot % 8 == 0) | (spot % 8 == 7)
    source = spot // 8 + jnp.where(spot % 8 == 7, 64, 0)
    for c in range(3):
        full = [dot(v[c], gr[...])]
        halves = [dot(v[c, :, 256 * h : 256 * h + 256], block[...]) for h in range(2)]
        for d in range(3):
            scale = scale_col(32, d)
            near = zs[3 * c + d]
            for t in range(4):
                lanes = slice(128 * t, 128 * t + 128)
                if d == 0:
                    raw = full[0][:, lanes]
                else:
                    at = 256 * (d - 1) + 128 * (t % 2)
                    raw = halves[t // 2][:, at : at + 128]
                raw = raw * scale
                mean = 0.5 * (raw + take_lanes(near, source + 16 * t))
                grad[3 * c + d, :, lanes] = jnp.where(on_face, mean, raw).astype(BF16)

    pltpu.make_async_copy(rret, rret, pr).wait()
    back = jnp.concatenate([rret[:, 0, :].T, rret[:, 1, :].T[0:64, :]], axis=0)
    hi, lo, _ = split3(back)
    rows = dot(jnp.concatenate([hi, lo], axis=1), hot2[...])
    for cc in range(12):
        pv[cc : cc + 1, :] = jnp.sum(rj[...] * rows[16 * cc : 16 * cc + 16, :], axis=0, keepdims=True)

    for copy in halo:
        copy.wait_send()
    for src, sem in ((sreq, qs), (sret, ps)):
        sent = src.at[pl.ds(0, NDEV - 1)]
        pltpu.make_async_copy(sent, sent, sem).wait()


def per_device(velocity, elem_scale, face_map, ref_coords, owner_dev, owner_elem):
    deriv = rounded_deriv()
    dtab = np.repeat(deriv.T, 128, axis=1).astype(np.float32)
    vmem = pl.BlockSpec(memory_space=pltpu.VMEM)
    out = pl.pallas_call(
        kernel,
        out_shape=(
            jax.ShapeDtypeStruct((9, 256, 512), BF16),
            jax.ShapeDtypeStruct((12, 1024), F32),
        ),
        in_specs=[vmem] * 12,
        out_specs=(vmem, vmem),
        scratch_shapes=[
            pltpu.VMEM((3, 256, 128), F32),
            pltpu.VMEM((3, 256, 128), F32),
            pltpu.VMEM((3, 256, 128), F32),
            pltpu.VMEM((3, 256, 128), F32),
            pltpu.VMEM((3, 256), F32),
            pltpu.VMEM((3, 256), F32),
            pltpu.VMEM((128, 128), jnp.int32),
            pltpu.VMEM((128, 128), jnp.int32),
            pltpu.VMEM((128, 1, 128), F32),
            pltpu.VMEM((128, 1, 128), F32),
            pltpu.VMEM((128, 2, 128), F32),
            pltpu.VMEM((128, 2, 128), F32),
            pltpu.VMEM((128, 128), F32),
            pltpu.VMEM((3, 512, 256), BF16),
            pltpu.VMEM((256, 2048), BF16),
            pltpu.VMEM((9, 256, 128), F32),
            pltpu.VMEM((384, 256), BF16),
            pltpu.VMEM((256, 128), F32),
            pltpu.VMEM((24, 2048), F32),
            pltpu.VMEM((16, 1024), F32),
            pltpu.VMEM((256, 1024), BF16),
            pltpu.VMEM((16, 256), F32),
            pltpu.VMEM((128, 128), F32),
            pltpu.VMEM((128, 128), F32),
            pltpu.SemaphoreType.DMA((9,)),
            pltpu.SemaphoreType.DMA((9,)),
            pltpu.SemaphoreType.DMA,
            pltpu.SemaphoreType.DMA,
            pltpu.SemaphoreType.DMA,
            pltpu.SemaphoreType.DMA,
            pltpu.SemaphoreType.REGULAR,
            pltpu.SemaphoreType.REGULAR,
        ],
        compiler_params=pltpu.CompilerParams(
            collective_id=0, has_side_effects=True, vmem_limit_bytes=56 * 1024 * 1024
        ),
    )(
        velocity.transpose(1, 0, 2),
        elem_scale.T,
        face_map.T,
        ref_coords,
        owner_dev.reshape(1, 1024),
        owner_elem.reshape(1, 1024),
        *tables(),
        jnp.asarray(dtab),
    )
    return out[0].transpose(1, 0, 2), out[1]


def solution(mesh):
    both = ("group", "member")
    in_specs = (P(both, None, None), P(both, None), P(both, None), P(None, both), P(both, None), P(both))
    out_specs = (P(both, None, None), P(None, both))
    return jax.shard_map(per_device, mesh=mesh, in_specs=in_specs, out_specs=out_specs, check_vma=False)
```

time: 183 us -> 50.6 us (0.28); the launches traced: 181 us -> 50.4 us
  local copies, waits for them, and re-layouts: 110 us -> 3.89 us
  Pallas kernels: 0 us -> 45.8 us
  matrix products: 21.1 us -> 0 us
  starting transfers between devices: 21 us -> 0 us
  other arithmetic: 15.7 us -> 0 us
  waiting for transfers between devices: 10.7 us -> 0 us
    gather x17 -> x0, local copies, waits for them, and re-layouts: 48.7 us -> none  [the longest x16 45.9 us: serve_block(): gathered = fields[element_ids].astype(jnp.float32)]
    pallas_call x0 -> x1, Pallas kernels: none -> 45.8 us  [per_device(): pl.pallas_call(kernel, out_shape=(jax.ShapeDtypeStruct((9, 256, 512), BF1...]
    dot_general x5 -> x0, matrix products: 21.1 us -> none  [the longest x1 8.75 us: per_device(): jnp.einsum('ecg,efg->ecf', top_prior, matcher, precision=lax.Precision.HI...]
    all_to_all x2 -> x0, starting transfers between devices: 13.4 us -> none  [the longest x1 6.93 us: per_device(): lax.all_to_all(results.transpose(1, 0, 2).reshape(12, sources, depth), ('...]
    dynamic_slice x16 -> x0, local copies, waits for them, and re-layouts: 11.9 us -> none  [per_device(): results = lax.map(serve_block, blocked)]
    all_to_all x2 -> x0, waiting for transfers between devices: 10.7 us -> none  [the longest x1 7.72 us: per_device(): lax.all_to_all(results.transpose(1, 0, 2).reshape(12, sources, depth), ('...]
    while x16 -> x0, other arithmetic: 8.35 us -> none
    unnamed x33 -> x4, local copies, waits for them, and re-layouts: 11.7 us -> 3.89 us
  transfers between devices with their start and end apart: 4 -> 0, of which waited for: 2 -> 0; matrix products, arithmetic and copies ran while one was open for 27% -> 0% of each run, Pallas kernels for 0% -> 0%
where the time goes in v1:
time: 50.6 us; the launch traced here: 50.4 us
  Pallas kernels  45.8 us (91%)
  local copies, waits for them, and re-layouts  3.89 us (8%)
  between operations  0.65 us (1%)
    pallas_call x1, Pallas kernels, per_device(): pl.pallas_call(kernel, out_shape=(jax.ShapeDtypeStruct((9, 256, 512), BF1...  45.8 us
    unnamed x4, local copies, waits for them, and re-layouts  3.89 us

profile of v1, /device:TPU:1, one launch (start us, length us, event | category | flops | bytes accessed | tf_op | source)
XLA Modules:
  0.0 50.4 jit_solution(858184124827412296)
XLA Ops:
  0.6 45.8 %shard_map.131 = (bf16[9,256,512]{2,1,0:T(8,128)(2,1)}, f32[12,1024]{1,0:T(8,128)}) custom-call(bf16[3,256,512]{2,1,0:T(8,128)(2,1)} %bitcast.7, f32[3,256]{1,0:T(4,128)} %bitcast.9, s32[64,256]{1,0:T(8,128)} %bitcast.8, f32[3,1024]{1,0:T(4,128)} %rc.1, s32[1,1024]{1,0:T(1,128)} %bitcast.10, s32[1,1024]{1,0:T(1,128)} %bitcast.11, ...), custom_call_target="tpu_custom_call" | custom-call | tf_op jit(solution)/shard_map/pallas_call | solution.py:349
  46.5 0.0 copy-start
  46.5 3.3 %copy.16 = bf16[256,9,512]{2,0,1:T(8,128)(2,1)} copy(bf16[256,9,512]{2,0,1:T(8,128)(2,1)} %bitcast.6) | data formatting | bytes 4718592
  49.7 0.0 copy-done
  49.7 0.6 %copy.17 = f32[12,1024]{1,0:T(8,128)} copy(f32[12,1024]{1,0:T(8,128)S(1)} %copy-done) | data formatting | bytes 98304
Async XLA Ops:
  46.5 3.3 %copy-start = (f32[12,1024]{1,0:T(8,128)S(1)}, f32[12,1024]{1,0:T(8,128)}, u32[]{:S(2)}) copy-start(f32[12,1024]{1,0:T(8,128)} %get-tuple-element.9) | copy-start | bytes 147460

commit v2 on v1

--- a/solution.py
+++ b/solution.py
@@ -97,14 +97,31 @@
     return out
 
 
-def kernel(v, sc, fm, rc, od, oe, face, gr, block, inner, count, dtab,
+def far_first():
+    hops = [0, 1, 2, 1]
+    every = [(x, y, z, c) for x in range(4) for y in range(4) for z in range(4) for c in range(2)]
+    every.remove((0, 0, 0, 0))
+    return sorted(every, key=lambda o: -(hops[o[0]] + hops[o[1]] + hops[o[2]]))
+
+
+def kernel(v_in, sc_in, fm_in, rc_in, od_in, oe_in, face_in, gr_in, block_in, inner_in, count_in, dtab_in,
            grad, pv,
+           v, sc, fm, rc, od, oe, face, gr, block, inner, count, dtab,
            topm, botm, rtop, rbot, scp, scn, invs, invr, sreq, rreq, sret, rret,
            scols, vt, hot, zs, zt, res, wts, rj, hot2, sclanes, rt, fmt,
-           hs, hr, qs, qr, ps, pr, sem_a, sem_b):
+           ins, hs, hr, qs, qr, ps, pr, sem_a, sem_b):
+    loads = {}
+    order = [("face", face_in, face), ("v0", v_in.at[0], v.at[0]), ("v1", v_in.at[1], v.at[1]),
+             ("v2", v_in.at[2], v.at[2]), ("sc", sc_in, sc), ("od", od_in, od), ("count", count_in, count),
+             ("rc", rc_in, rc), ("oe", oe_in, oe), ("fm", fm_in, fm), ("inner", inner_in, inner),
+             ("dtab", dtab_in, dtab), ("gr", gr_in, gr), ("block", block_in, block)]
+    for k, (name, src, dst) in enumerate(order):
+        loads[name] = pltpu.make_async_copy(src, dst, ins.at[k])
+        loads[name].start()
+
     g, m = lax.axis_index("group"), lax.axis_index("member")
     me = g * 16 + m
-    z, y = m // 4, m % 4
+    core, x, z, y = g % 2, g // 2, m // 4, m % 4
     nxt, prv = (me + 1) % NDEV, (me + NDEV - 1) % NDEV
     nxt, prv = (nxt // 16, nxt % 16), (prv // 16, prv % 16)
 
@@ -115,26 +132,54 @@
     for p in partners + zpart + ypart:
         pl.semaphore_signal(bar, inc=1, device_id=p, device_id_type=MESH)
 
+    loads["face"].wait()
     for c in range(3):
-        x = dot(v[c], face[...])
-        topm[c] = x[:, :128]
-        botm[c] = x[:, 128:]
-
-    fmt[0:64, :] = fm[:, 0:128].astype(F32)
-    fmt[64:128, :] = fm[:, 128:256].astype(F32)
-
-    def invert(f, acc):
-        lo, hi = acc
-        where = iota((64, 128), 0).astype(F32)
-        value = f.astype(F32)
-        lo = jnp.where(fmt[pl.ds(f, 1), :] == where, value, lo)
-        hi = jnp.where(fmt[pl.ds(64 + f, 1), :] == where, value, hi)
-        return lo, hi
-
-    zero = jnp.zeros((64, 128), F32)
-    inv_lo, inv_hi = lax.fori_loop(0, 64, invert, (zero, zero), unroll=8)
-    invs[...] = jnp.concatenate([inv_lo, inv_hi], axis=0).T.astype(jnp.int32)
-
+        loads["v%d" % c].wait()
+        out = dot(v[c], face[...])
+        topm[c] = out[:, :128]
+        botm[c] = out[:, 128:]
+    loads["sc"].wait()
+
+    pl.semaphore_wait(bar, len(partners) + 6)
+    for p in zpart:
+        pl.semaphore_signal(sem_a, inc=1, device_id=p, device_id_type=MESH)
+
+    def push(src, dst, k, to):
+        copy = pltpu.make_async_remote_copy(
+            src_ref=src, dst_ref=dst, send_sem=hs.at[k], recv_sem=hr.at[k], device_id=to, device_id_type=MESH
+        )
+        copy.start()
+        return copy
+
+    halo = [push(sc, scp, 0, nxt), push(sc, scn, 1, prv)]
+    for c in range(3):
+        halo.append(push(topm.at[c], rtop.at[c], 2 + 2 * c, nxt))
+        halo.append(push(botm.at[c], rbot.at[c], 3 + 2 * c, prv))
+        if c == 0:
+            loads["fm"].wait()
+            fmt[0:64, :] = fm[:, 0:128].astype(F32)
+            fmt[64:128, :] = fm[:, 128:256].astype(F32)
+
+            def invert(f, acc):
+                lo, hi = acc
+                where = iota((64, 128), 0).astype(F32)
+                value = f.astype(F32)
+                lo = jnp.where(fmt[pl.ds(f, 1), :] == where, value, lo)
+                hi = jnp.where(fmt[pl.ds(64 + f, 1), :] == where, value, hi)
+                return lo, hi
+
+            zero = jnp.zeros((64, 128), F32)
+            inv_lo, inv_hi = lax.fori_loop(0, 64, invert, (zero, zero), unroll=8)
+            invs[...] = jnp.concatenate([inv_lo, inv_hi], axis=0).T.astype(jnp.int32)
+            last = push(invs, invr, 8, prv)
+    halo.append(last)
+
+    pl.semaphore_wait(sem_a, 3)
+    for p in ypart:
+        pl.semaphore_signal(sem_b, inc=1, device_id=p, device_id_type=MESH)
+
+    for name in ("od", "count", "rc", "oe"):
+        loads[name].wait()
     running = jnp.zeros((128, 128), F32)
     for b in range(8):
         lanes = slice(128 * b, 128 * b + 128)
@@ -154,39 +199,16 @@
         send = one if send is None else send + one
     sreq[:, 0, :] = send
 
-    pl.semaphore_wait(bar, len(partners) + 6)
-    for p in zpart:
-        pl.semaphore_signal(sem_a, inc=1, device_id=p, device_id_type=MESH)
-
-    def push(src, dst, k, to):
-        copy = pltpu.make_async_remote_copy(
-            src_ref=src, dst_ref=dst, send_sem=hs.at[k], recv_sem=hr.at[k], device_id=to, device_id_type=MESH
-        )
-        copy.start()
-        return copy
-
-    halo = [push(sc, scp, 0, nxt), push(sc, scn, 1, prv), push(invs, invr, 2, prv)]
-    for c in range(3):
-        halo.append(push(topm.at[c], rtop.at[c], 3 + 2 * c, nxt))
-        halo.append(push(botm.at[c], rbot.at[c], 4 + 2 * c, prv))
-
-    pl.semaphore_wait(sem_a, 3)
-    for p in ypart:
-        pl.semaphore_signal(sem_b, inc=1, device_id=p, device_id_type=MESH)
     pl.semaphore_wait(sem_b, 3)
 
     def exchange(src, dst, ssem, rsem):
+        for ox, oy, oz, oc in far_first():
+            tg, tm = ((x + ox) % 4) * 2 + (core + oc) % 2, ((z + oz) % 4) * 4 + (y + oy) % 4
+            pltpu.make_async_remote_copy(
+                src_ref=src.at[tg * 16 + tm], dst_ref=dst.at[me], send_sem=ssem, recv_sem=rsem,
+                device_id=(tg, tm), device_id_type=MESH,
+            ).start()
         pltpu.make_async_copy(src.at[me], dst.at[me], rsem).start()
-
-        def one(i, carry):
-            t = (me + i) % NDEV
-            pltpu.make_async_remote_copy(
-                src_ref=src.at[t], dst_ref=dst.at[me], send_sem=ssem, recv_sem=rsem,
-                device_id=(t // 16, t % 16), device_id_type=MESH,
-            ).start()
-            return carry
-
-        lax.fori_loop(1, NDEV, one, 0)
 
     exchange(sreq, rreq, qs, qr)
 
@@ -196,6 +218,48 @@
         for i, part in enumerate(split3(sc[d : d + 1, :])):
             sclanes[3 * d + i : 3 * d + i + 1, :] = part.astype(F32)
     scales16 = jnp.concatenate([sclanes[0:9, :], jnp.zeros((7, 256), F32)], axis=0).astype(BF16)
+
+    for k in (0, 1, 8):
+        halo[k].wait_recv()
+    scols[...] = jnp.zeros((128, 128), F32)
+    for h in range(2):
+        lanes = slice(128 * h, 128 * h + 128)
+        scols[8 * h : 8 * h + 3, :] = scp[:, lanes]
+        scols[16 + 8 * h : 16 + 8 * h + 3, :] = scn[:, lanes]
+        scols[32 + 8 * h : 32 + 8 * h + 3, :] = sc[:, lanes]
+    cols = scols[...].T
+
+    def scale_col(base, d):
+        first = cols[:, base + d : base + d + 1]
+        second = cols[:, base + 8 + d : base + 8 + d + 1]
+        return jnp.concatenate([jnp.broadcast_to(first, (128, 128)), jnp.broadcast_to(second, (128, 128))], axis=0)
+
+    left = iota((256, 128), 1) < 64
+    both = [jnp.where(left, scale_col(0, d), scale_col(16, d)) for d in range(3)]
+    fm2, inv2 = fmt[...].T.astype(jnp.int32), invr[...]
+    left2 = iota((128, 128), 1) < 64
+    idx = jnp.concatenate(
+        [
+            jnp.where(left2, fm2, 64 + pltpu.roll(inv2, 64, 1)),
+            jnp.where(left2, pltpu.roll(fm2, 64, 1), 64 + inv2),
+        ],
+        axis=0,
+    )
+    loads["inner"].wait()
+    loads["dtab"].wait()
+
+    def build(c):
+        halo[2 + 2 * c].wait_recv()
+        halo[3 + 2 * c].wait_recv()
+        up, down = rtop[c], rbot[c]
+        rs = dot(jnp.concatenate([up, down], axis=1).astype(BF16), inner[...])
+        fields = [rs[:, :128], rs[:, 128:], jnp.where(left, pltpu.roll(up, 64, 1), down)]
+        for d in range(3):
+            turned = take_lanes(fields[d] * both[d], idx)
+            zs[3 * c + d] = turned
+            zt[384 * c + 128 * d : 384 * c + 128 * d + 128, :] = turned.T.astype(BF16)
+
+    build(0)
 
     pltpu.make_async_copy(rreq, rreq, qr).wait()
     rt[...] = rreq[:, 0, :].T
@@ -235,9 +299,9 @@
             for jj in range(8):
                 a0 = a1 = jnp.zeros((8, 256), F32)
                 for i in range(8):
-                    x = picked[64 * i + 8 * jj : 64 * i + 8 * jj + 8, :]
-                    a0 = a0 + lag[0][i : i + 1, :] * x
-                    a1 = a1 + der[0][i : i + 1, :] * x
+                    node = picked[64 * i + 8 * jj : 64 * i + 8 * jj + 8, :]
+                    a0 = a0 + lag[0][i : i + 1, :] * node
+                    a1 = a1 + der[0][i : i + 1, :] * node
                 s0 = s0 + lag[1][jj : jj + 1, :] * a0
                 s1 = s1 + der[1][jj : jj + 1, :] * a0
                 s2 = s2 + lag[1][jj : jj + 1, :] * a1
@@ -249,65 +313,32 @@
 
     lax.fori_loop(0, 8, own, 0)
 
-    for k in range(3):
-        halo[k].wait_recv()
-    scols[...] = jnp.zeros((128, 128), F32)
-    for h in range(2):
-        lanes = slice(128 * h, 128 * h + 128)
-        scols[8 * h : 8 * h + 3, :] = scp[:, lanes]
-        scols[16 + 8 * h : 16 + 8 * h + 3, :] = scn[:, lanes]
-        scols[32 + 8 * h : 32 + 8 * h + 3, :] = sc[:, lanes]
-    cols = scols[...].T
-
-    def scale_col(base, d):
-        first = cols[:, base + d : base + d + 1]
-        second = cols[:, base + 8 + d : base + 8 + d + 1]
-        return jnp.concatenate([jnp.broadcast_to(first, (128, 128)), jnp.broadcast_to(second, (128, 128))], axis=0)
-
-    left = iota((256, 128), 1) < 64
-    both = [jnp.where(left, scale_col(0, d), scale_col(16, d)) for d in range(3)]
-    fm2, inv2 = fmt[...].T.astype(jnp.int32), invr[...]
-    left2 = iota((128, 128), 1) < 64
-    idx = jnp.concatenate(
-        [
-            jnp.where(left2, fm2, 64 + pltpu.roll(inv2, 64, 1)),
-            jnp.where(left2, pltpu.roll(fm2, 64, 1), 64 + inv2),
-        ],
-        axis=0,
-    )
-
-    for c in range(3):
-        halo[3 + 2 * c].wait_recv()
-        halo[4 + 2 * c].wait_recv()
-        up, down = rtop[c], rbot[c]
-        rs = dot(jnp.concatenate([up, down], axis=1).astype(BF16), inner[...])
-        fields = [rs[:, :128], rs[:, 128:], jnp.where(left, pltpu.roll(up, 64, 1), down)]
-        for d in range(3):
-            turned = take_lanes(fields[d] * both[d], idx)
-            zs[3 * c + d] = turned
-            zt[128 * d : 128 * d + 128, :] = turned.T.astype(BF16)
-
-        def neighbours(j, carry):
-            lanes = pl.ds(pl.multiple_of(j * 256, 256), 256)
-            picked = dot(zt[...], hot[:, lanes])
-            lr, ls, lt = wts[0:8, lanes], wts[8:16, lanes], wts[16:24, lanes]
-            for d in range(3):
-                lo = hi = jnp.zeros((8, 256), F32)
-                for i in range(8):
-                    at = 128 * d + 8 * i
-                    lo = lo + lr[i : i + 1, :] * picked[at : at + 8, :]
-                    hi = hi + lr[i : i + 1, :] * picked[at + 64 : at + 72, :]
-                both_faces = 0.5 * (lt[0:1, :] * lo + lt[7:8, :] * hi)
-                put(3 + 3 * c + d, j, jnp.sum(ls * both_faces, axis=0, keepdims=True), True)
-            return carry
-
-        lax.fori_loop(0, 8, neighbours, 0)
+    build(1)
+    build(2)
+
+    def neighbours(j, carry):
+        lanes = pl.ds(pl.multiple_of(j * 256, 256), 256)
+        picked = dot(zt[...], hot[:, lanes])
+        lr, ls, lt = wts[0:8, lanes], wts[8:16, lanes], wts[16:24, lanes]
+        for cd in range(9):
+            lo = hi = jnp.zeros((8, 256), F32)
+            for i in range(8):
+                at = 128 * cd + 8 * i
+                lo = lo + lr[i : i + 1, :] * picked[at : at + 8, :]
+                hi = hi + lr[i : i + 1, :] * picked[at + 64 : at + 72, :]
+            both_faces = 0.5 * (lt[0:1, :] * lo + lt[7:8, :] * hi)
+            put(3 + cd, j, jnp.sum(ls * both_faces, axis=0, keepdims=True), True)
+        return carry
+
+    lax.fori_loop(0, 8, neighbours, 0)
 
     res[192:256, :] = jnp.zeros((64, 128), F32)
     sret[:, 0, :] = res[0:128, :].T
     sret[:, 1, :] = res[128:256, :].T
     exchange(sret, rret, ps, pr)
 
+    loads["gr"].wait()
+    loads["block"].wait()
     spot = iota((256, 128), 1)
     on_face = (spot % 8 == 0) | (spot % 8 == 7)
     source = spot // 8 + jnp.where(spot % 8 == 7, 64, 0)
@@ -352,9 +383,21 @@
             jax.ShapeDtypeStruct((9, 256, 512), BF16),
             jax.ShapeDtypeStruct((12, 1024), F32),
         ),
-        in_specs=[vmem] * 12,
+        in_specs=[pl.BlockSpec(memory_space=pltpu.HBM)] * 12,
         out_specs=(vmem, vmem),
         scratch_shapes=[
+            pltpu.VMEM((3, 256, 512), BF16),
+            pltpu.VMEM((3, 256), F32),
+            pltpu.VMEM((64, 256), jnp.int32),
+            pltpu.VMEM((3, 1024), F32),
+            pltpu.VMEM((1, 1024), jnp.int32),
+            pltpu.VMEM((1, 1024), jnp.int32),
+            pltpu.VMEM((512, 256), BF16),
+            pltpu.VMEM((512, 512), BF16),
+            pltpu.VMEM((256, 512), BF16),
+            pltpu.VMEM((256, 256), BF16),
+            pltpu.VMEM((128, 256), BF16),
+            pltpu.VMEM((8, 1024), F32),
             pltpu.VMEM((3, 256, 128), F32),
             pltpu.VMEM((3, 256, 128), F32),
             pltpu.VMEM((3, 256, 128), F32),
@@ -371,7 +414,7 @@
             pltpu.VMEM((3, 512, 256), BF16),
             pltpu.VMEM((256, 2048), BF16),
             pltpu.VMEM((9, 256, 128), F32),
-            pltpu.VMEM((384, 256), BF16),
+            pltpu.VMEM((1152, 256), BF16),
             pltpu.VMEM((256, 128), F32),
             pltpu.VMEM((24, 2048), F32),
             pltpu.VMEM((16, 1024), F32),
@@ -379,6 +422,7 @@
             pltpu.VMEM((16, 256), F32),
             pltpu.VMEM((128, 128), F32),
             pltpu.VMEM((128, 128), F32),
+            pltpu.SemaphoreType.DMA((14,)),
             pltpu.SemaphoreType.DMA((9,)),
             pltpu.SemaphoreType.DMA((9,)),
             pltpu.SemaphoreType.DMA,
@@ -389,17 +433,22 @@
             pltpu.SemaphoreType.REGULAR,
         ],
         compiler_params=pltpu.CompilerParams(
-            collective_id=0, has_side_effects=True, vmem_limit_bytes=56 * 1024 * 1024
+            collective_id=0, has_side_effects=True, vmem_limit_bytes=24 * 1024 * 1024
         ),
     )(
-        velocity.transpose(1, 0, 2),
-        elem_scale.T,
-        face_map.T,
-        ref_coords,
-        owner_dev.reshape(1, 1024),
-        owner_elem.reshape(1, 1024),
-        *tables(),
-        jnp.asarray(dtab),
+        *(
+            pltpu.with_memory_space_constraint(operand, pltpu.HBM)
+            for operand in (
+                velocity.transpose(1, 0, 2),
+                elem_scale.T,
+                face_map.T,
+                ref_coords,
+                owner_dev.reshape(1, 1024),
+                owner_elem.reshape(1, 1024),
+                *tables(),
+                jnp.asarray(dtab),
+            )
+        )
     )
     return out[0].transpose(1, 0, 2), out[1]
 

time: 50.6 us -> 40.7 us (0.80)
  Pallas kernels: 45.8 us -> 37.9 us
  local copies, waits for them, and re-layouts: 3.89 us -> 2.04 us
    pallas_call x1, Pallas kernels: 45.8 us -> 37.9 us  [per_device(): pl.pallas_call(kernel, out_shape=(jax.ShapeDtypeStruct((9, 256, 512), BF1...]
    unnamed x4 -> x2, local copies, waits for them, and re-layouts: 3.89 us -> 2.04 us
where the time goes in v2:
time: 40.7 us; the launch traced here: 40.6 us
  Pallas kernels  37.9 us (93%)
  local copies, waits for them, and re-layouts  2.04 us (5%)
  between operations  0.64 us (2%)
    pallas_call x1, Pallas kernels, per_device(): pl.pallas_call(kernel, out_shape=(jax.ShapeDtypeStruct((9, 256, 512), BF1...  37.9 us
    unnamed x2, local copies, waits for them, and re-layouts  2.04 us

profile of v2, /device:TPU:1, one launch (start us, length us, event | category | flops | bytes accessed | tf_op | source)
XLA Modules:
  0.0 40.6 jit_solution(11279288772719675162)
XLA Ops:
  0.6 37.9 %shard_map.131 = (bf16[9,256,512]{2,1,0:T(8,128)(2,1)S(1)}, f32[12,1024]{1,0:T(8,128)S(1)}) custom-call(bf16[3,256,512]{2,1,0:T(8,128)(2,1)} %bitcast.7, f32[3,256]{1,0:T(4,128)} %bitcast.9, s32[64,256]{1,0:T(8,128)} %bitcast.8, f32[3,1024]{1,0:T(4,128)} %rc_in.1, s32[1,1024]{1,0:T(1,128)} %bitcast.10, s32[1,1024]{1,0:T(1,128)} %bitcast.11, ...), custom_call_target="tpu_custom_call" | custom-call | tf_op jit(solution)/shard_map/pallas_call | solution.py:380
  38.6 1.4 %copy.16 = bf16[256,9,512]{2,0,1:T(8,128)(2,1)} copy(bf16[256,9,512]{2,0,1:T(8,128)(2,1)S(1)} %bitcast.6) | data formatting | bytes 4718592
  40.0 0.6 %copy.17 = f32[12,1024]{1,0:T(8,128)} copy(f32[12,1024]{1,0:T(8,128)S(1)} %get-tuple-element.9) | data formatting | bytes 98304

commit v3 on v2

--- a/solution.py
+++ b/solution.py
@@ -10,7 +10,8 @@
 
 MESH = pl.DeviceIdType.MESH
 F32, BF16 = jnp.float32, jnp.bfloat16
-NDEV, CAP = 128, 16
+NDEV = 128
+EARLY = 1
 
 
 def gll_nodes():
@@ -140,6 +141,22 @@
         botm[c] = out[:, 128:]
     loads["sc"].wait()
 
+    loads["fm"].wait()
+    fmt[0:64, :] = fm[:, 0:128].astype(F32)
+    fmt[64:128, :] = fm[:, 128:256].astype(F32)
+
+    def invert(f, acc):
+        lo, hi = acc
+        where = iota((64, 128), 0).astype(F32)
+        value = f.astype(F32)
+        lo = jnp.where(fmt[pl.ds(f, 1), :] == where, value, lo)
+        hi = jnp.where(fmt[pl.ds(64 + f, 1), :] == where, value, hi)
+        return lo, hi
+
+    zero = jnp.zeros((64, 128), F32)
+    inv_lo, inv_hi = lax.fori_loop(0, 64, invert, (zero, zero), unroll=8)
+    invs[...] = jnp.concatenate([inv_lo, inv_hi], axis=0).T.astype(jnp.int32)
+
     pl.semaphore_wait(bar, len(partners) + 6)
     for p in zpart:
         pl.semaphore_signal(sem_a, inc=1, device_id=p, device_id_type=MESH)
@@ -151,28 +168,14 @@
         copy.start()
         return copy
 
-    halo = [push(sc, scp, 0, nxt), push(sc, scn, 1, prv)]
-    for c in range(3):
-        halo.append(push(topm.at[c], rtop.at[c], 2 + 2 * c, nxt))
-        halo.append(push(botm.at[c], rbot.at[c], 3 + 2 * c, prv))
-        if c == 0:
-            loads["fm"].wait()
-            fmt[0:64, :] = fm[:, 0:128].astype(F32)
-            fmt[64:128, :] = fm[:, 128:256].astype(F32)
-
-            def invert(f, acc):
-                lo, hi = acc
-                where = iota((64, 128), 0).astype(F32)
-                value = f.astype(F32)
-                lo = jnp.where(fmt[pl.ds(f, 1), :] == where, value, lo)
-                hi = jnp.where(fmt[pl.ds(64 + f, 1), :] == where, value, hi)
-                return lo, hi
-
-            zero = jnp.zeros((64, 128), F32)
-            inv_lo, inv_hi = lax.fori_loop(0, 64, invert, (zero, zero), unroll=8)
-            invs[...] = jnp.concatenate([inv_lo, inv_hi], axis=0).T.astype(jnp.int32)
-            last = push(invs, invr, 8, prv)
-    halo.append(last)
+    halo = {0: push(sc, scp, 0, nxt), 1: push(sc, scn, 1, prv)}
+
+    def push_faces(c):
+        halo[2 + 2 * c] = push(topm.at[c], rtop.at[c], 2 + 2 * c, nxt)
+        halo[3 + 2 * c] = push(botm.at[c], rbot.at[c], 3 + 2 * c, prv)
+
+    for c in range(EARLY):
+        push_faces(c)
 
     pl.semaphore_wait(sem_a, 3)
     for p in ypart:
@@ -211,6 +214,9 @@
         pltpu.make_async_copy(src.at[me], dst.at[me], rsem).start()
 
     exchange(sreq, rreq, qs, qr)
+    halo[8] = push(invs, invr, 8, prv)
+    for c in range(EARLY, 3):
+        push_faces(c)
 
     for c in range(3):
         vt[c] = v[c].astype(F32).T.astype(BF16)
@@ -311,7 +317,7 @@
                 put(3 + 3 * c + d, j, jnp.sum(part, axis=0, keepdims=True) * scale, False)
         return carry
 
-    lax.fori_loop(0, 8, own, 0)
+    lax.fori_loop(0, 8, own, 0, unroll=8)
 
     build(1)
     build(2)
@@ -330,7 +336,7 @@
             put(3 + cd, j, jnp.sum(ls * both_faces, axis=0, keepdims=True), True)
         return carry
 
-    lax.fori_loop(0, 8, neighbours, 0)
+    lax.fori_loop(0, 8, neighbours, 0, unroll=8)
 
     res[192:256, :] = jnp.zeros((64, 128), F32)
     sret[:, 0, :] = res[0:128, :].T
@@ -366,7 +372,7 @@
     for cc in range(12):
         pv[cc : cc + 1, :] = jnp.sum(rj[...] * rows[16 * cc : 16 * cc + 16, :], axis=0, keepdims=True)
 
-    for copy in halo:
+    for copy in halo.values():
         copy.wait_send()
     for src, sem in ((sreq, qs), (sret, ps)):
         sent = src.at[pl.ds(0, NDEV - 1)]

time: 40.7 us -> 34.8 us (0.86)
  Pallas kernels: 37.9 us -> 32 us
    pallas_call x1, Pallas kernels: 37.9 us -> 32 us  [per_device(): pl.pallas_call(kernel, out_shape=(jax.ShapeDtypeStruct((9, 256, 512), BF1...]
where the time goes in v3:
time: 34.8 us; the launch traced here: 34.7 us
  Pallas kernels  32 us (92%)
  local copies, waits for them, and re-layouts  2.04 us (6%)
  between operations  0.64 us (2%)
    pallas_call x1, Pallas kernels, per_device(): pl.pallas_call(kernel, out_shape=(jax.ShapeDtypeStruct((9, 256, 512), BF1...  32 us
    unnamed x2, local copies, waits for them, and re-layouts  2.04 us

profile of v3, /device:TPU:1, one launch (start us, length us, event | category | flops | bytes accessed | tf_op | source)
XLA Modules:
  0.0 34.7 jit_solution(12386750271983620389)
XLA Ops:
  0.6 32.0 %shard_map.131 = (bf16[9,256,512]{2,1,0:T(8,128)(2,1)S(1)}, f32[12,1024]{1,0:T(8,128)S(1)}) custom-call(bf16[3,256,512]{2,1,0:T(8,128)(2,1)} %bitcast.7, f32[3,256]{1,0:T(4,128)} %bitcast.9, s32[64,256]{1,0:T(8,128)} %bitcast.8, f32[3,1024]{1,0:T(4,128)} %rc_in.1, s32[1,1024]{1,0:T(1,128)} %bitcast.10, s32[1,1024]{1,0:T(1,128)} %bitcast.11, ...), custom_call_target="tpu_custom_call" | custom-call | tf_op jit(solution)/shard_map/pallas_call | solution.py:386
  32.7 1.4 %copy.16 = bf16[256,9,512]{2,0,1:T(8,128)(2,1)} copy(bf16[256,9,512]{2,0,1:T(8,128)(2,1)S(1)} %bitcast.6) | data formatting | bytes 4718592
  34.1 0.6 %copy.17 = f32[12,1024]{1,0:T(8,128)} copy(f32[12,1024]{1,0:T(8,128)S(1)} %get-tuple-element.9) | data formatting | bytes 98304

commit v4 on v3

--- a/solution.py
+++ b/solution.py
@@ -11,7 +11,7 @@
 MESH = pl.DeviceIdType.MESH
 F32, BF16 = jnp.float32, jnp.bfloat16
 NDEV = 128
-EARLY = 1
+EARLY_TOP, EARLY_BOTTOM = 2, 2
 
 
 def gll_nodes():
@@ -106,10 +106,10 @@
 
 
 def kernel(v_in, sc_in, fm_in, rc_in, od_in, oe_in, face_in, gr_in, block_in, inner_in, count_in, dtab_in,
-           grad, pv,
+           grad, back, rj, hot2,
            v, sc, fm, rc, od, oe, face, gr, block, inner, count, dtab,
            topm, botm, rtop, rbot, scp, scn, invs, invr, sreq, rreq, sret, rret,
-           scols, vt, hot, zs, zt, res, wts, rj, hot2, sclanes, rt, fmt,
+           scols, vt, hot, zs, zt, res, wts, sclanes, rt, fmt,
            ins, hs, hr, qs, qr, ps, pr, sem_a, sem_b):
     loads = {}
     order = [("face", face_in, face), ("v0", v_in.at[0], v.at[0]), ("v1", v_in.at[1], v.at[1]),
@@ -170,13 +170,18 @@
 
     halo = {0: push(sc, scp, 0, nxt), 1: push(sc, scn, 1, prv)}
 
-    def push_faces(c):
-        halo[2 + 2 * c] = push(topm.at[c], rtop.at[c], 2 + 2 * c, nxt)
-        halo[3 + 2 * c] = push(botm.at[c], rbot.at[c], 3 + 2 * c, prv)
-
-    for c in range(EARLY):
-        push_faces(c)
-
+    def push_top(k):
+        c, rows = k // 2, pl.ds(128 * (k % 2), 128)
+        halo[3 + k] = push(topm.at[c, rows], rtop.at[c, rows], 3 + k, nxt)
+
+    def push_bottom(k):
+        c, rows = k // 2, pl.ds(128 * (k % 2), 128)
+        halo[9 + k] = push(botm.at[c, rows], rbot.at[c, rows], 9 + k, prv)
+
+    for k in range(EARLY_TOP):
+        push_top(k)
+        if k < EARLY_BOTTOM:
+            push_bottom(k)
     pl.semaphore_wait(sem_a, 3)
     for p in ypart:
         pl.semaphore_signal(sem_b, inc=1, device_id=p, device_id_type=MESH)
@@ -214,9 +219,11 @@
         pltpu.make_async_copy(src.at[me], dst.at[me], rsem).start()
 
     exchange(sreq, rreq, qs, qr)
-    halo[8] = push(invs, invr, 8, prv)
-    for c in range(EARLY, 3):
-        push_faces(c)
+    halo[2] = push(invs, invr, 2, prv)
+    for k in range(EARLY_BOTTOM, 6):
+        push_bottom(k)
+        if k >= EARLY_TOP:
+            push_top(k)
 
     for c in range(3):
         vt[c] = v[c].astype(F32).T.astype(BF16)
@@ -225,7 +232,7 @@
             sclanes[3 * d + i : 3 * d + i + 1, :] = part.astype(F32)
     scales16 = jnp.concatenate([sclanes[0:9, :], jnp.zeros((7, 256), F32)], axis=0).astype(BF16)
 
-    for k in (0, 1, 8):
+    for k in (0, 1, 2):
         halo[k].wait_recv()
     scols[...] = jnp.zeros((128, 128), F32)
     for h in range(2):
@@ -255,8 +262,9 @@
     loads["dtab"].wait()
 
     def build(c):
-        halo[2 + 2 * c].wait_recv()
-        halo[3 + 2 * c].wait_recv()
+        for k in (2 * c, 2 * c + 1):
+            halo[3 + k].wait_recv()
+            halo[9 + k].wait_recv()
         up, down = rtop[c], rbot[c]
         rs = dot(jnp.concatenate([up, down], axis=1).astype(BF16), inner[...])
         fields = [rs[:, :128], rs[:, 128:], jnp.where(left, pltpu.roll(up, 64, 1), down)]
@@ -319,24 +327,27 @@
 
     lax.fori_loop(0, 8, own, 0, unroll=8)
 
+    def neighbours(first, number):
+        def body(j, carry):
+            lanes = pl.ds(pl.multiple_of(j * 256, 256), 256)
+            picked = dot(zt[384 * first : 384 * (first + number), :], hot[:, lanes])
+            lr, ls, lt = wts[0:8, lanes], wts[8:16, lanes], wts[16:24, lanes]
+            for cd in range(3 * number):
+                lo = hi = jnp.zeros((8, 256), F32)
+                for i in range(8):
+                    at = 128 * cd + 8 * i
+                    lo = lo + lr[i : i + 1, :] * picked[at : at + 8, :]
+                    hi = hi + lr[i : i + 1, :] * picked[at + 64 : at + 72, :]
+                both_faces = 0.5 * (lt[0:1, :] * lo + lt[7:8, :] * hi)
+                put(3 + 3 * first + cd, j, jnp.sum(ls * both_faces, axis=0, keepdims=True), True)
+            return carry
+
+        lax.fori_loop(0, 8, body, 0, unroll=8)
+
     build(1)
+    neighbours(0, 2)
     build(2)
-
-    def neighbours(j, carry):
-        lanes = pl.ds(pl.multiple_of(j * 256, 256), 256)
-        picked = dot(zt[...], hot[:, lanes])
-        lr, ls, lt = wts[0:8, lanes], wts[8:16, lanes], wts[16:24, lanes]
-        for cd in range(9):
-            lo = hi = jnp.zeros((8, 256), F32)
-            for i in range(8):
-                at = 128 * cd + 8 * i
-                lo = lo + lr[i : i + 1, :] * picked[at : at + 8, :]
-                hi = hi + lr[i : i + 1, :] * picked[at + 64 : at + 72, :]
-            both_faces = 0.5 * (lt[0:1, :] * lo + lt[7:8, :] * hi)
-            put(3 + cd, j, jnp.sum(ls * both_faces, axis=0, keepdims=True), True)
-        return carry
-
-    lax.fori_loop(0, 8, neighbours, 0, unroll=8)
+    neighbours(2, 1)
 
     res[192:256, :] = jnp.zeros((64, 128), F32)
     sret[:, 0, :] = res[0:128, :].T
@@ -366,17 +377,26 @@
                 grad[3 * c + d, :, lanes] = jnp.where(on_face, mean, raw).astype(BF16)
 
     pltpu.make_async_copy(rret, rret, pr).wait()
-    back = jnp.concatenate([rret[:, 0, :].T, rret[:, 1, :].T[0:64, :]], axis=0)
-    hi, lo, _ = split3(back)
-    rows = dot(jnp.concatenate([hi, lo], axis=1), hot2[...])
-    for cc in range(12):
-        pv[cc : cc + 1, :] = jnp.sum(rj[...] * rows[16 * cc : 16 * cc + 16, :], axis=0, keepdims=True)
+    back[...] = rret[...]
 
     for copy in halo.values():
         copy.wait_send()
     for src, sem in ((sreq, qs), (sret, ps)):
         sent = src.at[pl.ds(0, NDEV - 1)]
         pltpu.make_async_copy(sent, sent, sem).wait()
+
+
+def finish(grad, back, rj, hot2, grad_out, pv, sem):
+    copies = [pltpu.make_async_copy(grad.at[k], grad_out.at[k], sem.at[k]) for k in range(9)]
+    for copy in copies:
+        copy.start()
+    table = jnp.concatenate([back[:, 0, :].T, back[:, 1, :].T[0:64, :]], axis=0)
+    hi, lo, _ = split3(table)
+    rows = dot(jnp.concatenate([hi, lo], axis=1), hot2[...])
+    for cc in range(12):
+        pv[cc : cc + 1, :] = jnp.sum(rj[...] * rows[16 * cc : 16 * cc + 16, :], axis=0, keepdims=True)
+    for copy in copies:
+        copy.wait()
 
 
 def per_device(velocity, elem_scale, face_map, ref_coords, owner_dev, owner_elem):
@@ -387,10 +407,12 @@
         kernel,
         out_shape=(
             jax.ShapeDtypeStruct((9, 256, 512), BF16),
-            jax.ShapeDtypeStruct((12, 1024), F32),
+            jax.ShapeDtypeStruct((128, 2, 128), F32),
+            jax.ShapeDtypeStruct((16, 1024), F32),
+            jax.ShapeDtypeStruct((256, 1024), BF16),
         ),
         in_specs=[pl.BlockSpec(memory_space=pltpu.HBM)] * 12,
-        out_specs=(vmem, vmem),
+        out_specs=(vmem,) * 4,
         scratch_shapes=[
             pltpu.VMEM((3, 256, 512), BF16),
             pltpu.VMEM((3, 256), F32),
@@ -423,14 +445,12 @@
             pltpu.VMEM((1152, 256), BF16),
             pltpu.VMEM((256, 128), F32),
             pltpu.VMEM((24, 2048), F32),
-            pltpu.VMEM((16, 1024), F32),
-            pltpu.VMEM((256, 1024), BF16),
             pltpu.VMEM((16, 256), F32),
             pltpu.VMEM((128, 128), F32),
             pltpu.VMEM((128, 128), F32),
             pltpu.SemaphoreType.DMA((14,)),
-            pltpu.SemaphoreType.DMA((9,)),
-            pltpu.SemaphoreType.DMA((9,)),
+            pltpu.SemaphoreType.DMA((15,)),
+            pltpu.SemaphoreType.DMA((15,)),
             pltpu.SemaphoreType.DMA,
             pltpu.SemaphoreType.DMA,
             pltpu.SemaphoreType.DMA,
@@ -456,7 +476,15 @@
             )
         )
     )
-    return out[0].transpose(1, 0, 2), out[1]
+    grad, values = pl.pallas_call(
+        finish,
+        out_shape=(jax.ShapeDtypeStruct((9, 256, 512), BF16), jax.ShapeDtypeStruct((12, 1024), F32)),
+        in_specs=[vmem] * 4,
+        out_specs=(pl.BlockSpec(memory_space=pltpu.HBM), vmem),
+        scratch_shapes=[pltpu.SemaphoreType.DMA((9,))],
+        compiler_params=pltpu.CompilerParams(vmem_limit_bytes=16 * 1024 * 1024),
+    )(*out)
+    return grad.transpose(1, 0, 2), values
 
 
 def solution(mesh):

time: 34.8 us -> 34.2 us (0.983)
  local copies, waits for them, and re-layouts: 2.04 us -> 0 us
  Pallas kernels: 32 us -> 33.4 us
    pallas_call x0 -> x1, Pallas kernels: none -> 2.18 us  [per_device(): pl.pallas_call(finish, out_shape=(jax.ShapeDtypeStruct((9, 256, 512), BF1...]
    unnamed x2 -> x0, local copies, waits for them, and re-layouts: 2.04 us -> none
    pallas_call x1, Pallas kernels: 32 us -> 31.2 us  [per_device(): pl.pallas_call(kernel, out_shape=(jax.ShapeDtypeStruct((9, 256, 512), BF1...]
where the time goes in v4:
time: 34.2 us; the launch traced here: 34 us
  Pallas kernels  33.4 us (98%)
  between operations  0.64 us (2%)
    pallas_call x1, Pallas kernels, per_device(): pl.pallas_call(kernel, out_shape=(jax.ShapeDtypeStruct((9, 256, 512), BF1...  31.2 us
    pallas_call x1, Pallas kernels, per_device(): pl.pallas_call(finish, out_shape=(jax.ShapeDtypeStruct((9, 256, 512), BF1...  2.18 us

profile of v4, /device:TPU:1, one launch (start us, length us, event | category | flops | bytes accessed | tf_op | source)
XLA Modules:
  0.0 34.0 jit_solution(5908503672922990511)
XLA Ops:
  0.6 31.2 %shard_map.131 = (bf16[9,256,512]{2,1,0:T(8,128)(2,1)S(1)}, f32[128,2,128]{2,1,0:T(2,128)S(1)}, f32[16,1024]{1,0:T(8,128)S(1)}, bf16[256,1024]{1,0:T(8,128)(2,1)S(1)}) custom-call(bf16[3,256,512]{2,1,0:T(8,128)(2,1)} %bitcast.6, f32[3,256]{1,0:T(4,128)} %bitcast.8, s32[64,256]{1,0:T(8,128)} %bitcast.7, f32[3,1024]{1,0:T(4,128)} %rc_in.1, s32[1,1024]{1,0:T(1,128)} %bitcast.9, ...), custom_call_target="tpu_custom_call" | custom-call | tf_op jit(solution)/shard_map/pallas_call | solution.py:406
  31.8 2.2 %shard_map.132 = (bf16[9,256,512]{2,1,0:T(8,128)(2,1)}, f32[12,1024]{1,0:T(8,128)}) custom-call(bf16[9,256,512]{2,1,0:T(8,128)(2,1)S(1)} %get-tuple-element.8.grad, f32[128,2,128]{2,1,0:T(2,128)S(1)} %get-tuple-element.9.back, f32[16,1024]{1,0:T(8,128)S(1)} %get-tuple-element.10.rj, bf16[256,1024]{1,0:T(8,128)(2,1)S(1)} %get-tuple-element.11.hot2), custom_call_target="tpu_custom_call" | custom-call | tf_op jit(solution)/shard_map/pallas_call | solution.py:479

commit v5 on v4

--- a/solution.py
+++ b/solution.py
@@ -386,7 +386,7 @@
         pltpu.make_async_copy(sent, sent, sem).wait()
 
 
-def finish(grad, back, rj, hot2, grad_out, pv, sem):
+def finish(grad, back, rj, hot2, grad_out, pv_out, pv, sem):
     copies = [pltpu.make_async_copy(grad.at[k], grad_out.at[k], sem.at[k]) for k in range(9)]
     for copy in copies:
         copy.start()
@@ -395,7 +395,9 @@
     rows = dot(jnp.concatenate([hi, lo], axis=1), hot2[...])
     for cc in range(12):
         pv[cc : cc + 1, :] = jnp.sum(rj[...] * rows[16 * cc : 16 * cc + 16, :], axis=0, keepdims=True)
-    for copy in copies:
+    last = pltpu.make_async_copy(pv, pv_out, sem.at[9])
+    last.start()
+    for copy in copies + [last]:
         copy.wait()
 
 
@@ -480,8 +482,8 @@
         finish,
         out_shape=(jax.ShapeDtypeStruct((9, 256, 512), BF16), jax.ShapeDtypeStruct((12, 1024), F32)),
         in_specs=[vmem] * 4,
-        out_specs=(pl.BlockSpec(memory_space=pltpu.HBM), vmem),
-        scratch_shapes=[pltpu.SemaphoreType.DMA((9,))],
+        out_specs=(pl.BlockSpec(memory_space=pltpu.HBM),) * 2,
+        scratch_shapes=[pltpu.VMEM((12, 1024), F32), pltpu.SemaphoreType.DMA((10,))],
         compiler_params=pltpu.CompilerParams(vmem_limit_bytes=16 * 1024 * 1024),
     )(*out)
     return grad.transpose(1, 0, 2), values

time: 34.2 us -> 33.5 us (0.980)
  Pallas kernels: 33.4 us -> 32.8 us
    pallas_call x1, Pallas kernels: 2.18 us -> 1.56 us  [per_device(): pl.pallas_call(finish, out_shape=(jax.ShapeDtypeStruct((9, 256, 512), BF1...]
where the time goes in v5:
time: 33.5 us; the launch traced here: 33.4 us
  Pallas kernels  32.8 us (98%)
  between operations  0.64 us (2%)
    pallas_call x1, Pallas kernels, per_device(): pl.pallas_call(kernel, out_shape=(jax.ShapeDtypeStruct((9, 256, 512), BF1...  31.2 us
    pallas_call x1, Pallas kernels, per_device(): pl.pallas_call(finish, out_shape=(jax.ShapeDtypeStruct((9, 256, 512), BF1...  1.56 us

profile of v5, /device:TPU:1, one launch (start us, length us, event | category | flops | bytes accessed | tf_op | source)
XLA Modules:
  0.0 33.4 jit_solution(7187880350012133847)
XLA Ops:
  0.6 31.2 %shard_map.131 = (bf16[9,256,512]{2,1,0:T(8,128)(2,1)S(1)}, f32[128,2,128]{2,1,0:T(2,128)S(1)}, f32[16,1024]{1,0:T(8,128)S(1)}, bf16[256,1024]{1,0:T(8,128)(2,1)S(1)}) custom-call(bf16[3,256,512]{2,1,0:T(8,128)(2,1)} %bitcast.6, f32[3,256]{1,0:T(4,128)} %bitcast.8, s32[64,256]{1,0:T(8,128)} %bitcast.7, f32[3,1024]{1,0:T(4,128)} %rc_in.1, s32[1,1024]{1,0:T(1,128)} %bitcast.9, ...), custom_call_target="tpu_custom_call" | custom-call | tf_op jit(solution)/shard_map/pallas_call | solution.py:408
  31.8 1.6 %shard_map.132 = (bf16[9,256,512]{2,1,0:T(8,128)(2,1)}, f32[12,1024]{1,0:T(8,128)}) custom-call(bf16[9,256,512]{2,1,0:T(8,128)(2,1)S(1)} %get-tuple-element.8.grad, f32[128,2,128]{2,1,0:T(2,128)S(1)} %get-tuple-element.9.back, f32[16,1024]{1,0:T(8,128)S(1)} %get-tuple-element.10.rj, bf16[256,1024]{1,0:T(8,128)(2,1)S(1)} %get-tuple-element.11.hot2), custom_call_target="tpu_custom_call" | custom-call | tf_op jit(solution)/shard_map/pallas_call | solution.py:481

commit v6 on v5

--- a/solution.py
+++ b/solution.py
@@ -11,7 +11,7 @@
 MESH = pl.DeviceIdType.MESH
 F32, BF16 = jnp.float32, jnp.bfloat16
 NDEV = 128
-EARLY_TOP, EARLY_BOTTOM = 2, 2
+EARLY_TOP, EARLY_BOTTOM = 1, 1
 
 
 def gll_nodes():
@@ -171,12 +171,10 @@
     halo = {0: push(sc, scp, 0, nxt), 1: push(sc, scn, 1, prv)}
 
     def push_top(k):
-        c, rows = k // 2, pl.ds(128 * (k % 2), 128)
-        halo[3 + k] = push(topm.at[c, rows], rtop.at[c, rows], 3 + k, nxt)
+        halo[3 + k] = push(topm.at[k], rtop.at[k], 3 + k, nxt)
 
     def push_bottom(k):
-        c, rows = k // 2, pl.ds(128 * (k % 2), 128)
-        halo[9 + k] = push(botm.at[c, rows], rbot.at[c, rows], 9 + k, prv)
+        halo[6 + k] = push(botm.at[k], rbot.at[k], 6 + k, prv)
 
     for k in range(EARLY_TOP):
         push_top(k)
@@ -220,7 +218,7 @@
 
     exchange(sreq, rreq, qs, qr)
     halo[2] = push(invs, invr, 2, prv)
-    for k in range(EARLY_BOTTOM, 6):
+    for k in range(EARLY_BOTTOM, 3):
         push_bottom(k)
         if k >= EARLY_TOP:
             push_top(k)
@@ -262,9 +260,8 @@
     loads["dtab"].wait()
 
     def build(c):
-        for k in (2 * c, 2 * c + 1):
-            halo[3 + k].wait_recv()
-            halo[9 + k].wait_recv()
+        halo[3 + c].wait_recv()
+        halo[6 + c].wait_recv()
         up, down = rtop[c], rbot[c]
         rs = dot(jnp.concatenate([up, down], axis=1).astype(BF16), inner[...])
         fields = [rs[:, :128], rs[:, 128:], jnp.where(left, pltpu.roll(up, 64, 1), down)]
@@ -344,8 +341,9 @@
 
         lax.fori_loop(0, 8, body, 0, unroll=8)
 
+    neighbours(0, 1)
     build(1)
-    neighbours(0, 2)
+    neighbours(1, 1)
     build(2)
     neighbours(2, 1)
 
@@ -451,8 +449,8 @@
             pltpu.VMEM((128, 128), F32),
             pltpu.VMEM((128, 128), F32),
             pltpu.SemaphoreType.DMA((14,)),
-            pltpu.SemaphoreType.DMA((15,)),
-            pltpu.SemaphoreType.DMA((15,)),
+            pltpu.SemaphoreType.DMA((9,)),
+            pltpu.SemaphoreType.DMA((9,)),
             pltpu.SemaphoreType.DMA,
             pltpu.SemaphoreType.DMA,
             pltpu.SemaphoreType.DMA,

time: 33.5 us -> 33.5 us (level)
  no operation moved by 1% of the time
where the time goes in v6:
time: 33.5 us; the launch traced here: 33.3 us
  Pallas kernels  32.7 us (98%)
  between operations  0.64 us (2%)
    pallas_call x1, Pallas kernels, per_device(): pl.pallas_call(kernel, out_shape=(jax.ShapeDtypeStruct((9, 256, 512), BF1...  31.1 us
    pallas_call x1, Pallas kernels, per_device(): pl.pallas_call(finish, out_shape=(jax.ShapeDtypeStruct((9, 256, 512), BF1...  1.56 us

profile of v6, /device:TPU:1, one launch (start us, length us, event | category | flops | bytes accessed | tf_op | source)
XLA Modules:
  0.0 33.3 jit_solution(15488890057907656704)
XLA Ops:
  0.6 31.1 %shard_map.131 = (bf16[9,256,512]{2,1,0:T(8,128)(2,1)S(1)}, f32[128,2,128]{2,1,0:T(2,128)S(1)}, f32[16,1024]{1,0:T(8,128)S(1)}, bf16[256,1024]{1,0:T(8,128)(2,1)S(1)}) custom-call(bf16[3,256,512]{2,1,0:T(8,128)(2,1)} %bitcast.6, f32[3,256]{1,0:T(4,128)} %bitcast.8, s32[64,256]{1,0:T(8,128)} %bitcast.7, f32[3,1024]{1,0:T(4,128)} %rc_in.1, s32[1,1024]{1,0:T(1,128)} %bitcast.9, ...), custom_call_target="tpu_custom_call" | custom-call | tf_op jit(solution)/shard_map/pallas_call | solution.py:406
  31.8 1.6 %shard_map.132 = (bf16[9,256,512]{2,1,0:T(8,128)(2,1)}, f32[12,1024]{1,0:T(8,128)}) custom-call(bf16[9,256,512]{2,1,0:T(8,128)(2,1)S(1)} %get-tuple-element.8.grad, f32[128,2,128]{2,1,0:T(2,128)S(1)} %get-tuple-element.9.back, f32[16,1024]{1,0:T(8,128)S(1)} %get-tuple-element.10.rj, bf16[256,1024]{1,0:T(8,128)(2,1)S(1)} %get-tuple-element.11.hot2), custom_call_target="tpu_custom_call" | custom-call | tf_op jit(solution)/shard_map/pallas_call | solution.py:479
